TPU v7x, 32 devices: a whole 2x2x4 slice. The times are simulated.
32 devices in a mesh: rep: 8 (over y, x, core), shard: 4 (over z).
Axes of the slice: x: 2, y: 2, z: 4, core: 2. Of those that a mesh axis runs over, the one named last changes fastest.
Arguments:
- queries: bfloat16 [4096, 4096], P(('rep', 'shard')), may hold values from -120 to 120
- keys: bfloat16 [4096, 512], P(('rep', 'shard')), may hold values from -5.5 to 5.5
- grad_out: bfloat16 [4096, 4096], P(('rep', 'shard')), may hold values from -3 to 3
- inputs: bfloat16 [4096, 8192], P(('rep', 'shard')), may hold values from -6 to 6
- old_owner: int32 [64], replicated, may hold values from 0 to 2, as said below
- new_owner: int32 [64], replicated, may hold values from 0 to 3, as said below
- param_old: float32 [128, 88, 512], P('rep', 'shard'), may hold values from -0.75 to 0.75
- first_old: float32 [128, 88, 512], P('rep', 'shard'), may hold values from -6 to 6
- second_old: float32 [128, 88, 512], P('rep', 'shard'), may hold values from 0.5 to 20
Outputs:
- param_new: float32 [128, 64, 512], P('rep', 'shard')
- first_new: float32 [128, 64, 512], P('rep', 'shard')
- second_new: float32 [128, 64, 512], P('rep', 'shard')
- weights: bfloat16 [128, 64, 512], P('rep')
Inputs may be any that keep to these rules, and one draw needn't show every extreme that they name: `old_owner`: each old owner holds at most 22 blocks, and some hold exactly 22. `new_owner`: each new owner holds exactly 16 blocks.
All inputs are finite; a program needn't handle non-finite values.
Results may differ from a plain program's by a relative error of at most 0.0034.
Values may be sent and summed in bfloat16 or wider, within the bound.
A program may use at most 128 MiB of HBM per device.

v0:
```python
import jax
import jax.numpy as jnp
from jax import lax
from jax.sharding import PartitionSpec as P

KV = 4
HD = 128
GRP = 8
STEP = 1000
beta_first = 0.9
beta_second = 0.95
learning_rate = 0.02
decay_rate = 0.1
epsilon = 1e-08


def owner_ranks(owner, owners):
    onehot = (owner[:, None] == jnp.arange(owners, dtype=jnp.int32)[None, :]).astype(jnp.int32)
    running = jnp.cumsum(onehot, axis=0)
    return jnp.sum(running * onehot, axis=1) - 1


def slot_table(owner, owners, capacity):
    blocks = owner.shape[0]
    position = owner * capacity + owner_ranks(owner, owners)
    match = position[None, :] == jnp.arange(owners * capacity, dtype=jnp.int32)[:, None]
    chosen = jnp.sum(jnp.where(match, jnp.arange(blocks, dtype=jnp.int32)[None, :], 0), axis=1)
    return (chosen, jnp.any(match, axis=1))


def adamw(param, first, second, gradient):
    first = beta_first * first + (1.0 - beta_first) * gradient
    second = beta_second * second + (1.0 - beta_second) * gradient * gradient
    first_hat = first / (1.0 - beta_first**STEP)
    second_hat = second / (1.0 - beta_second**STEP)
    param = param - learning_rate * (
        first_hat / (jnp.sqrt(second_hat) + epsilon) + decay_rate * param
    )
    return (param, first, second)


def value_terms(queries, keys_all, grad_out, offset):
    rows_here = queries.shape[0]
    length = keys_all.shape[0]
    query_groups = queries.reshape(rows_here, KV, GRP, HD).transpose(1, 2, 0, 3)
    cotangent_groups = grad_out.reshape(rows_here, KV, GRP, HD).transpose(1, 2, 0, 3)
    key_groups = keys_all.reshape(length, KV, HD).transpose(1, 0, 2)
    allowed = jnp.arange(length)[None, :] <= (offset + jnp.arange(rows_here))[:, None]

    def one_group(triple):
        query_block, key_block, cotangent = triple
        scores = jnp.einsum(
            "htd,ud->htu", query_block, key_block, preferred_element_type=jnp.float32
        ) * HD ** (-0.5)
        scores = jnp.where(allowed[None], scores, -jnp.inf)
        highest = jnp.max(scores, axis=-1, keepdims=True)
        weights = jnp.exp(scores - highest)
        probs = (weights / jnp.sum(weights, axis=-1, keepdims=True)).astype(jnp.bfloat16)
        return jnp.einsum("htu,htd->ud", probs, cotangent, preferred_element_type=jnp.float32)

    return lax.map(one_group, (query_groups, key_groups, cotangent_groups))


def local(queries, keys, grad_out, inputs, old_owner, new_owner, param_old, first_old, second_old):
    shards = lax.axis_size("shard")
    replicas = lax.axis_size("rep")
    shard_index = lax.axis_index("shard")
    rows_here = queries.shape[0]
    blocks = old_owner.shape[0]
    block_rows = inputs.shape[1] // blocks
    old_capacity = param_old.shape[1]
    new_capacity = blocks // shards
    columns = KV * HD
    keys_all = lax.all_gather(keys, "shard", axis=0, tiled=True)
    value_part = value_terms(queries, keys_all, grad_out, shard_index * rows_here)
    values = lax.psum(value_part, "shard").astype(jnp.bfloat16)
    slot_block, slot_valid = slot_table(new_owner, shards, new_capacity)
    pieces = inputs.reshape(rows_here, blocks, block_rows)
    outgoing = jnp.where(
        slot_valid[None, :, None], jnp.take(pieces, slot_block, axis=1), jnp.zeros((), jnp.bfloat16)
    )
    arrived = lax.all_to_all(outgoing, "shard", split_axis=1, concat_axis=0, tiled=True)
    product = jnp.einsum("tsk,gtd->ksgd", arrived, values, preferred_element_type=jnp.float32)
    gradient = lax.psum_scatter(
        product.reshape(block_rows // replicas * lax.axis_size("rep"), new_capacity, columns),
        "rep",
        scatter_dimension=0,
        tiled=True,
    )
    new_block, unused_valid = slot_table(new_owner, shards, new_capacity)
    old_rank = owner_ranks(old_owner, shards)
    gathered = (
        lax.all_gather(param_old, "shard", axis=1, tiled=True),
        lax.all_gather(first_old, "shard", axis=1, tiled=True),
        lax.all_gather(second_old, "shard", axis=1, tiled=True),
    )
    my_blocks = lax.dynamic_slice_in_dim(new_block, shard_index * new_capacity, new_capacity)
    source = jnp.take(old_owner, my_blocks) * old_capacity + jnp.take(old_rank, my_blocks)
    moved = tuple((jnp.take(state, source, axis=1) for state in gathered))
    param_new, first_new, second_new = adamw(moved[0], moved[1], moved[2], gradient)
    working = param_new.astype(jnp.bfloat16)
    every_shard = lax.all_gather(working, "shard", axis=1, tiled=True)
    new_slot = new_owner * new_capacity + owner_ranks(new_owner, shards)
    weights = jnp.take(every_shard, new_slot, axis=1)
    return (param_new, first_new, second_new, weights)


def solution(mesh):
    placed = (
        P(("rep", "shard"), None),
        P(("rep", "shard"), None),
        P(("rep", "shard"), None),
        P(("rep", "shard"), None),
        P(),
        P(),
        P("rep", "shard", None),
        P("rep", "shard", None),
        P("rep", "shard", None),
    )
    return jax.shard_map(
        local,
        mesh=mesh,
        in_specs=placed,
        out_specs=(
            P("rep", "shard", None),
            P("rep", "shard", None),
            P("rep", "shard", None),
            P("rep", None, None),
        ),
        check_vma=False,
    )
```

profile of v0, /device:TPU:0, one launch (start us, length us, event | category | flops | bytes accessed | tf_op | source)
XLA Modules:
  0.0 316.6 jit_solution(666578656723029522)
XLA Ops:
  9.5 3.2 %copy.75 = bf16[128,8192]{0,1:T(8,128)(2,1)S(1)} copy(bf16[128,8192]{1,0:T(8,128)(2,1)} %param.18) | data formatting | bytes 4194304 | tf_op args[3]
  12.7 2.9 copy.76
  16.2 2.5 gather_fusion
  18.8 1.7 select_bitcast_fusion
  20.5 6.5 %all-to-all-start = ((bf16[128,64,128]{2,0,1:T(8,128)(2,1)}), bf16[128,64,128]{2,0,1:T(8,128)(2,1)S(1)}, u32[]{:S(2)}, u32[]{:S(2)}) async-start(bf16[128,64,128]{2,0,1:T(8,128)(2,1)} %select_bitcast_fusion), calls=%async_computation | async-start | bytes 4194304 | tf_op jit(solution)/shard_map/all_to_all | solution.py:82
  27.8 1.3 copy.68
  29.3 2.4 copy.70
  31.6 94.6 %all_gather.17 = bf16[512,512]{0,1:T(8,128)(2,1)} all-gather(bf16[128,512]{0,1:T(8,128)(2,1)S(1)} %copy.69), channel_id=1, replica_groups=mesh['rep'=8,'shard'=4] {'shard'}, dimensions={0}, use_global_device_ids=true | all-gather | bytes 655360 | tf_op jit(solution)/shard_map/all_gather | solution.py:74
  126.2 22.7 %while.11 = (s32[]{:T(128)}, f32[4,512,128]{1,2,0:T(8,128)}, bf16[4,8,128,128]{2,3,1,0:T(8,128)(2,1)S(1)}, bf16[4,512,128]{1,2,0:T(8,128)(2,1)}, bf16[4,8,128,12...) while((s32[]{:T(128)}, f32[4,512,128]{1,2,0:T(8,128)}, ...), condition=%wide.region_8.11_spmd.clone, body=%wide.region_5.0_spmd.clone.sunk | while | flops 407439360 | bytes 1519189 | solution.py:61
  126.3 1.8 fusion.78
  128.1 3.8 %fusion.79 = f32[4,512,128]{1,2,0:T(8,128)} fusion(f32[4,512,128]{1,2,0:T(8,128)} %get-tuple-element.159, s32[]{:T(128)S(6)} %copy.96, f32[8,128]{1,0:T(8,128)S(1)} %fusion.78, bf16[4,8,128,128]{2,3,1,0:T(8,128)(2,1)} %get-tuple-element.169, pred[128,512]{1,0:T(8,128)(4,1)S(1)} %iota_compare_fusion.5, ...), kind=kOutput, calls=%fused_computation.14.clone.1 | convolution fusion | flops 271058432 | bytes 989184 | tf_op jit(solution)/shard_map/while/body/eval_jaxpr/htu,htd->ud/dot_general | solution.py:59
  132.0 1.8 fusion.78
  133.8 3.8 %fusion.79 = f32[4,512,128]{1,2,0:T(8,128)} fusion(f32[4,512,128]{1,2,0:T(8,128)} %get-tuple-element.159, s32[]{:T(128)S(6)} %copy.96, f32[8,128]{1,0:T(8,128)S(1)} %fusion.78, bf16[4,8,128,128]{2,3,1,0:T(8,128)(2,1)} %get-tuple-element.169, pred[128,512]{1,0:T(8,128)(4,1)S(1)} %iota_compare_fusion.5, ...), kind=kOutput, calls=%fused_computation.14.clone.1 | convolution fusion | flops 271058432 | bytes 989184 | tf_op jit(solution)/shard_map/while/body/eval_jaxpr/htu,htd->ud/dot_general | solution.py:59
  137.6 1.8 fusion.78
  139.4 3.8 %fusion.79 = f32[4,512,128]{1,2,0:T(8,128)} fusion(f32[4,512,128]{1,2,0:T(8,128)} %get-tuple-element.159, s32[]{:T(128)S(6)} %copy.96, f32[8,128]{1,0:T(8,128)S(1)} %fusion.78, bf16[4,8,128,128]{2,3,1,0:T(8,128)(2,1)} %get-tuple-element.169, pred[128,512]{1,0:T(8,128)(4,1)S(1)} %iota_compare_fusion.5, ...), kind=kOutput, calls=%fused_computation.14.clone.1 | convolution fusion | flops 271058432 | bytes 989184 | tf_op jit(solution)/shard_map/while/body/eval_jaxpr/htu,htd->ud/dot_general | solution.py:59
  143.3 1.8 fusion.78
  145.1 3.8 %fusion.79 = f32[4,512,128]{1,2,0:T(8,128)} fusion(f32[4,512,128]{1,2,0:T(8,128)} %get-tuple-element.159, s32[]{:T(128)S(6)} %copy.96, f32[8,128]{1,0:T(8,128)S(1)} %fusion.78, bf16[4,8,128,128]{2,3,1,0:T(8,128)(2,1)} %get-tuple-element.169, pred[128,512]{1,0:T(8,128)(4,1)S(1)} %iota_compare_fusion.5, ...), kind=kOutput, calls=%fused_computation.14.clone.1 | convolution fusion | flops 271058432 | bytes 989184 | tf_op jit(solution)/shard_map/while/body/eval_jaxpr/htu,htd->ud/dot_general | solution.py:59
  148.9 65.2 %all-reduce.1 = bf16[4,512,128]{1,2,0:T(8,128)(2,1)S(1)} all-reduce(f32[4,512,128]{1,2,0:T(8,128)} %get-tuple-element.38), channel_id=1, replica_groups=mesh['rep'=8,'shard'=4] {'shard'}, use_global_device_ids=true, to_apply=%region_9.12 | all-reduce | flops 262144 | bytes 1572864 | tf_op jit(solution)/shard_map/psum | solution.py:76
  214.3 1.3 convolution_bitcast_fusion.1
  215.5 2.2 copy.79
  217.8 5.4 %copy.80 = f32[128,16,512]{2,0,1:T(8,128)} copy(f32[128,16,512]{0,2,1:T(8,128)} %bitcast.107) | data formatting | bytes 8388608 | tf_op jit(solution)/shard_map/reshape | solution.py:85
  225.7 2.4 gather_fusion.4
  228.1 2.4 gather_fusion.6
  230.6 29.3 %all-gather.7.cloned.1.call-done = f32[16,88,512]{2,0,1:T(8,128)} async-done(((f32[16,22,512]{2,0,1:T(8,128)}), f32[16,88,512]{2,0,1:T(8,128)}) %all-gather.7.cloned.1.call-update) | async-done | bytes 2883600 | tf_op jit(solution)/shard_map/all_gather | solution.py:94
  259.8 2.4 gather_fusion.5
  262.3 13.2 %reduce-scatter.2.cloned.1.call-done = f32[16,16,512]{2,0,1:T(8,128)} async-done(((f32[128,16,512]{2,0,1:T(8,128)}), f32[16,16,512]{2,0,1:T(8,128)}) %reduce-scatter.2.cloned.1.call-update) | async-done | bytes 524304 | tf_op jit(solution)/shard_map/reduce_scatter | solution.py:84
  275.5 2.2 fusion.57
  277.8 1.1 copy.81
  278.9 1.1 copy.82
  281.1 24.8 %all-gather.11.cloned.1.call-done = bf16[16,64,512]{2,0,1:T(8,128)(2,1)} async-done(((bf16[16,16,512]{2,0,1:T(8,128)(2,1)}), bf16[16,64,512]{2,0,1:T(8,128)(2,1)}) %all-gather.11.cloned.1.call-update) | async-done | bytes 1048592 | tf_op jit(solution)/shard_map/all_gather | solution.py:102
  305.9 1.8 gather_fusion.1
  307.9 1.5 copy.84
  (54 shorter events, 7.3 us)
Async XLA Ops:
  8.0 217.7 %all-gather.5.cloned.1.call-start = ((), (), s32[]{:S(2)}) async-start(), calls=%async_computation.2 | async-start | bytes 3604480 | tf_op jit(solution)/shard_map/all_gather | solution.py:93
  8.7 219.4 %all-gather.9.cloned.1.call-start = ((), (), s32[]{:S(2)}) async-start(), calls=%async_computation.5 | async-start | bytes 3604480 | tf_op jit(solution)/shard_map/all_gather | solution.py:95
  12.7 2.9 copy-start.4
  20.5 7.3 %copy-start.1 = (bf16[128,4096]{1,0:T(8,128)(2,1)S(1)}, bf16[128,4096]{1,0:T(8,128)(2,1)}, u32[]{:S(2)}) copy-start(bf16[128,4096]{1,0:T(8,128)(2,1)} %param.15) | copy-start | bytes 3145732
  20.5 193.6 %all-to-all-start = ((bf16[128,64,128]{2,0,1:T(8,128)(2,1)}), bf16[128,64,128]{2,0,1:T(8,128)(2,1)S(1)}, u32[]{:S(2)}, u32[]{:S(2)}) async-start(bf16[128,64,128]{2,0,1:T(8,128)(2,1)} %select_bitcast_fusion), calls=%async_computation | async-start | bytes 4194304 | tf_op jit(solution)/shard_map/all_to_all | solution.py:82
  27.0 2.1 copy-start.3
  27.0 232.8 %all-gather.7.cloned.1.call-start = ((), (), s32[]{:S(2)}) async-start(), calls=%async_computation.3 | async-start | bytes 3604480 | tf_op jit(solution)/shard_map/all_gather | solution.py:94
  27.7 247.8 %reduce-scatter.2.cloned.1.call-start = ((), (), s32[]{:S(2)}) async-start(), calls=%async_computation.4 | async-start | bytes 4718592 | tf_op jit(solution)/shard_map/reduce_scatter | solution.py:84
  29.1 97.0 %copy-start.2 = (bf16[128,4096]{0,1:T(8,128)(2,1)S(1)}, bf16[128,4096]{0,1:T(8,128)(2,1)}, u32[]{:S(2)}) copy-start(bf16[128,4096]{0,1:T(8,128)(2,1)} %copy.68) | copy-start | bytes 3145732
  223.1 0.7 copy-start
  223.2 82.7 %all-gather.11.cloned.1.call-start = ((), (), s32[]{:S(2)}) async-start(), calls=%async_computation.6 | async-start | bytes 1310720 | tf_op jit(solution)/shard_map/all_gather | solution.py:102
Sparse Core Ops, SparseCore 0:
  10.4 110.3 all-gather.4
  122.3 77.7 all-gather.8
  201.6 58.1 all-gather.6
  277.9 27.9 all-gather.10
Sparse Core Ops, SparseCore 1:
  223.2 52.2 reduce-scatter.1
where the time goes:
time: 317 us
  blocking collectives  160 us (50%)
  waiting for transfers between devices  69.5 us (22%)
  local copies, waits for them, and re-layouts  36.1 us (11%)
  matrix products  23.5 us (7%)
  between operations  15.4 us (5%)
  starting transfers between devices  6.64 us (2%)
  other arithmetic  5.65 us (2%)
    all_gather x1, blocking collectives, local(): keys_all = lax.all_gather(keys, 'shard', axis=0, tiled=True)  94.6 us
    psum x1, blocking collectives, local(): values = lax.psum(value_part, 'shard').astype(jnp.bfloat16)  65.2 us
    all_gather x1, waiting for transfers between devices, local(): lax.all_gather(first_old, 'shard', axis=1, tiled=True)  29.3 us
    all_gather x1, waiting for transfers between devices, local(): every_shard = lax.all_gather(working, 'shard', axis=1, tiled=True)  24.8 us
    dot_general x4, matrix products, one_group(): jnp.einsum('htu,htd->ud', probs, cotangent, preferred_element_type=jnp.fl...  15.1 us
    reduce_scatter x1, waiting for transfers between devices, local(): lax.psum_scatter(product.reshape(block_rows // replicas * lax.axis_size('...  13.2 us
    unnamed x18, local copies, waits for them, and re-layouts  12.5 us
    gather x3, local copies, waits for them, and re-layouts, local(): moved = tuple((jnp.take(state, source, axis=1) for state in gathered))  7.27 us
  transfers between devices with their start and end apart: 6, of which 3 were waited for; matrix products, arithmetic and copies ran while one was open for 19% of the time, Pallas kernels for 0%

commit v1 on v0

--- a/solution.py
+++ b/solution.py
@@ -71,7 +71,14 @@
     old_capacity = param_old.shape[1]
     new_capacity = blocks // shards
     columns = KV * HD
-    keys_all = lax.all_gather(keys, "shard", axis=0, tiled=True)
+    ring = [keys]
+    for hop in range(3):
+        ring.append(lax.ppermute(ring[-1], "shard", [(dev, (dev + 1) % 4) for dev in range(4)]))
+    keys_all = jnp.roll(
+        jnp.concatenate(ring[::-1], axis=0),
+        (lax.axis_index("shard") + 1) * ring[0].shape[0],
+        axis=0,
+    )
     value_part = value_terms(queries, keys_all, grad_out, shard_index * rows_here)
     values = lax.psum(value_part, "shard").astype(jnp.bfloat16)
     slot_block, slot_valid = slot_table(new_owner, shards, new_capacity)

time: 317 us -> 305 us (0.962)
  blocking collectives: 160 us -> 113 us
  waiting for transfers between devices: 69.5 us -> 94.6 us
  local copies, waits for them, and re-layouts: 36.1 us -> 40.2 us
    all_gather x1 -> x0, blocking collectives: 94.6 us -> none  [local(): keys_all = lax.all_gather(keys, 'shard', axis=0, tiled=True)]
    all_gather x1, waiting for transfers between devices: 0.02 us -> 58.2 us  [local(): lax.all_gather(param_old, 'shard', axis=1, tiled=True)]
    psum x1, blocking collectives: 65.2 us -> 113 us  [local(): values = lax.psum(value_part, 'shard').astype(jnp.bfloat16)]
    all_gather x1, waiting for transfers between devices: 29.3 us -> 0.02 us  [local(): lax.all_gather(first_old, 'shard', axis=1, tiled=True)]
    reduce_scatter x1, waiting for transfers between devices: 13.2 us -> 0.03 us  [local(): lax.psum_scatter(product.reshape(block_rows // replicas * lax.axis_size('...]
    all_gather x1, waiting for transfers between devices: 0.02 us -> 7.73 us  [local(): lax.all_gather(second_old, 'shard', axis=1, tiled=True)]
    ppermute x0 -> x3, starting transfers between devices: none -> 4.48 us  [local(): lax.ppermute(ring[-1], 'shard', [(dev, (dev + 1) % 4) for dev in range(4)])]
    unnamed x18 -> x21, local copies, waits for them, and re-layouts: 12.5 us -> 15.5 us
  transfers between devices with their start and end apart: 6 -> 9, of which waited for: 3 -> 4; matrix products, arithmetic and copies ran while one was open for 19% -> 21% of each run, Pallas kernels for 0% -> 0%
where the time goes in v1:
time: 305 us; the launch traced here: 304 us
  blocking collectives  113 us (37%)
  waiting for transfers between devices  94.6 us (31%)
  local copies, waits for them, and re-layouts  40.2 us (13%)
  matrix products  23.4 us (8%)
  between operations  15.5 us (5%)
  starting transfers between devices  9.08 us (3%)
  other arithmetic  7.61 us (2%)
    psum x1, blocking collectives, local(): values = lax.psum(value_part, 'shard').astype(jnp.bfloat16)  113 us
    all_gather x1, waiting for transfers between devices, local(): lax.all_gather(param_old, 'shard', axis=1, tiled=True)  58.2 us
    all_gather x1, waiting for transfers between devices, local(): every_shard = lax.all_gather(working, 'shard', axis=1, tiled=True)  23.5 us
    unnamed x21, local copies, waits for them, and re-layouts  15.5 us
    dot_general x4, matrix products, one_group(): jnp.einsum('htu,htd->ud', probs, cotangent, preferred_element_type=jnp.fl...  15.1 us
    all_gather x1, waiting for transfers between devices, local(): lax.all_gather(second_old, 'shard', axis=1, tiled=True)  7.73 us
    gather x3, local copies, waits for them, and re-layouts, local(): moved = tuple((jnp.take(state, source, axis=1) for state in gathered))  7.46 us
    sub x4, matrix products, one_group(): weights = jnp.exp(scores - highest)  7.13 us
  transfers between devices with their start and end apart: 9, of which 4 were waited for; matrix products, arithmetic and copies ran while one was open for 21% of the time, Pallas kernels for 0%

profile of v1, /device:TPU:0, one launch (start us, length us, event | category | flops | bytes accessed | tf_op | source)
XLA Modules:
  0.0 303.9 jit_solution(15267992031843604643)
XLA Ops:
  10.5 3.1 %collective-permute-start = (bf16[128,512]{0,1:T(8,128)(2,1)S(1)}, bf16[128,512]{0,1:T(8,128)(2,1)S(1)}, u32[]{:S(2)}, u32[]{:S(2)}) collective-permute-start(bf16[128,512]{0,1:T(8,128)(2,1)S(1)} %copy.75), channel_id=1, source_target_pairs={{0,1},{1,2},{2,3},{3,0},{4,5},{5,6},{6,7},{7,4},{8,9},{9,10},{10,1... | collective-permute-start | bytes 393224 | tf_op jit(solution)/shard_map/ppermute | solution.py:76
  16.1 3.1 %collective-permute-done = bf16[128,512]{0,1:T(8,128)(2,1)S(1)} collective-permute-done((bf16[128,512]{0,1:T(8,128)(2,1)S(1)}, bf16[128,512]{0,1:T(8,128)(2,1)S(1)}, u32[]{:S(2)}, u32[]{:S(2)}) %collective-permute-start) | collective-permute-done | bytes 131104 | tf_op jit(solution)/shard_map/ppermute | solution.py:76
  19.1 3.3 %copy.83 = bf16[128,8192]{0,1:T(8,128)(2,1)S(1)} copy(bf16[128,8192]{1,0:T(8,128)(2,1)} %param.18) | data formatting | bytes 4194304 | tf_op args[3]
  22.5 2.9 copy.84
  25.4 2.5 gather_fusion
  28.0 1.4 collective-permute-start.2
  29.4 1.7 select_bitcast_fusion
  31.1 4.4 %all-to-all-start = ((bf16[128,64,128]{2,0,1:T(8,128)(2,1)}), bf16[128,64,128]{2,0,1:T(8,128)(2,1)S(1)}, u32[]{:S(2)}, u32[]{:S(2)}) async-start(bf16[128,64,128]{2,0,1:T(8,128)(2,1)} %select_bitcast_fusion), calls=%async_computation | async-start | bytes 4194304 | tf_op jit(solution)/shard_map/all_to_all | solution.py:89
  36.4 1.3 copy.74
  37.7 2.3 copy.78
  43.1 22.6 %while.11 = (s32[]{:T(128)}, f32[4,512,128]{1,2,0:T(8,128)}, bf16[4,8,128,128]{2,3,1,0:T(8,128)(2,1)S(1)}, bf16[4,512,128]{1,2,0:T(8,128)(2,1)}, bf16[4,8,128,12...) while((s32[]{:T(128)}, f32[4,512,128]{1,2,0:T(8,128)}, ...), condition=%wide.region_8.11_spmd.clone, body=%wide.region_5.10_spmd.clone.sunk | while | flops 407439360 | bytes 1519181 | solution.py:61
  43.2 1.8 fusion.78
  45.0 3.8 %fusion.79 = f32[4,512,128]{1,2,0:T(8,128)} fusion(f32[4,512,128]{1,2,0:T(8,128)} %get-tuple-element.159, s32[]{:T(128)} %get-tuple-element.158, f32[8,128]{1,0:T(8,128)S(1)} %fusion.78, bf16[4,8,128,128]{2,3,1,0:T(8,128)(2,1)} %get-tuple-element.169, pred[128,512]{1,0:T(8,128)(4,1)S(1)} %iota_compare_fusion.5, ...), kind=kOutput, calls=%fused_computation.14.clone.1 | convolution fusion | flops 271058432 | bytes 989184 | tf_op jit(solution)/shard_map/while/body/eval_jaxpr/htu,htd->ud/dot_general | solution.py:59
  48.8 1.8 fusion.78
  50.6 3.8 %fusion.79 = f32[4,512,128]{1,2,0:T(8,128)} fusion(f32[4,512,128]{1,2,0:T(8,128)} %get-tuple-element.159, s32[]{:T(128)} %get-tuple-element.158, f32[8,128]{1,0:T(8,128)S(1)} %fusion.78, bf16[4,8,128,128]{2,3,1,0:T(8,128)(2,1)} %get-tuple-element.169, pred[128,512]{1,0:T(8,128)(4,1)S(1)} %iota_compare_fusion.5, ...), kind=kOutput, calls=%fused_computation.14.clone.1 | convolution fusion | flops 271058432 | bytes 989184 | tf_op jit(solution)/shard_map/while/body/eval_jaxpr/htu,htd->ud/dot_general | solution.py:59
  54.5 1.8 fusion.78
  56.3 3.8 %fusion.79 = f32[4,512,128]{1,2,0:T(8,128)} fusion(f32[4,512,128]{1,2,0:T(8,128)} %get-tuple-element.159, s32[]{:T(128)} %get-tuple-element.158, f32[8,128]{1,0:T(8,128)S(1)} %fusion.78, bf16[4,8,128,128]{2,3,1,0:T(8,128)(2,1)} %get-tuple-element.169, pred[128,512]{1,0:T(8,128)(4,1)S(1)} %iota_compare_fusion.5, ...), kind=kOutput, calls=%fused_computation.14.clone.1 | convolution fusion | flops 271058432 | bytes 989184 | tf_op jit(solution)/shard_map/while/body/eval_jaxpr/htu,htd->ud/dot_general | solution.py:59
  60.2 1.8 fusion.78
  61.9 3.8 %fusion.79 = f32[4,512,128]{1,2,0:T(8,128)} fusion(f32[4,512,128]{1,2,0:T(8,128)} %get-tuple-element.159, s32[]{:T(128)} %get-tuple-element.158, f32[8,128]{1,0:T(8,128)S(1)} %fusion.78, bf16[4,8,128,128]{2,3,1,0:T(8,128)(2,1)} %get-tuple-element.169, pred[128,512]{1,0:T(8,128)(4,1)S(1)} %iota_compare_fusion.5, ...), kind=kOutput, calls=%fused_computation.14.clone.1 | convolution fusion | flops 271058432 | bytes 989184 | tf_op jit(solution)/shard_map/while/body/eval_jaxpr/htu,htd->ud/dot_general | solution.py:59
  65.7 113.4 %all-reduce.1 = bf16[4,512,128]{1,2,0:T(8,128)(2,1)S(1)} all-reduce(f32[4,512,128]{1,2,0:T(8,128)} %get-tuple-element.38), channel_id=1, replica_groups=mesh['rep'=8,'shard'=4] {'shard'}, use_global_device_ids=true, to_apply=%region_9.12 | all-reduce | flops 262144 | bytes 1572864 | tf_op jit(solution)/shard_map/psum | solution.py:83
  179.3 1.3 convolution_bitcast_fusion.1
  180.6 2.2 copy.87
  182.8 5.4 %copy.88 = f32[128,16,512]{2,0,1:T(8,128)} copy(f32[128,16,512]{0,2,1:T(8,128)} %bitcast.107) | data formatting | bytes 8388608 | tf_op jit(solution)/shard_map/reshape | solution.py:92
  190.7 2.4 gather_fusion.5
  193.1 7.7 %all-gather.9.cloned.1.call-done = f32[16,88,512]{2,0,1:T(8,128)} async-done(((f32[16,22,512]{2,0,1:T(8,128)}), f32[16,88,512]{2,0,1:T(8,128)}) %all-gather.9.cloned.1.call-update) | async-done | bytes 2883600 | tf_op jit(solution)/shard_map/all_gather | solution.py:102
  200.9 2.7 gather_fusion.6
  203.6 58.2 %all-gather.5.cloned.1.call-done = f32[16,88,512]{2,0,1:T(8,128)} async-done(((f32[16,22,512]{2,0,1:T(8,128)}), f32[16,88,512]{2,0,1:T(8,128)}) %all-gather.5.cloned.1.call-update) | async-done | bytes 2883600 | tf_op jit(solution)/shard_map/all_gather | solution.py:100
  261.7 2.4 gather_fusion.4
  264.2 2.2 fusion.57
  269.8 23.5 %all-gather.11.cloned.1.call-done = bf16[16,64,512]{2,0,1:T(8,128)(2,1)} async-done(((bf16[16,16,512]{2,0,1:T(8,128)(2,1)}), bf16[16,64,512]{2,0,1:T(8,128)(2,1)}) %all-gather.11.cloned.1.call-update) | async-done | bytes 1048592 | tf_op jit(solution)/shard_map/all_gather | solution.py:109
  293.2 1.8 gather_fusion.1
  295.3 1.5 copy.92
  (64 shorter events, 15.4 us)
Async XLA Ops:
  8.0 182.7 %all-gather.7.cloned.1.call-start = ((), (), s32[]{:S(2)}) async-start(), calls=%async_computation.3 | async-start | bytes 3604480 | tf_op jit(solution)/shard_map/all_gather | solution.py:101
  8.7 192.1 %all-gather.9.cloned.1.call-start = ((), (), s32[]{:S(2)}) async-start(), calls=%async_computation.5 | async-start | bytes 3604480 | tf_op jit(solution)/shard_map/all_gather | solution.py:102
  10.5 8.6 %collective-permute-start = (bf16[128,512]{0,1:T(8,128)(2,1)S(1)}, bf16[128,512]{0,1:T(8,128)(2,1)S(1)}, u32[]{:S(2)}, u32[]{:S(2)}) collective-permute-start(bf16[128,512]{0,1:T(8,128)(2,1)S(1)} %copy.75), channel_id=1, source_target_pairs={{0,1},{1,2},{2,3},{3,0},{4,5},{5,6},{6,7},{7,4},{8,9},{9,10},{10,1... | collective-permute-start | bytes 393224 | tf_op jit(solution)/shard_map/ppermute | solution.py:76
  19.1 8.9 %collective-permute-start.1 = (bf16[128,512]{0,1:T(8,128)(2,1)S(1)}, bf16[128,512]{0,1:T(8,128)(2,1)S(1)}, u32[]{:S(2)}, u32[]{:S(2)}) collective-permute-start(bf16[128,512]{0,1:T(8,128)(2,1)S(1)} %collective-permute-done), channel_id=1, source_target_pairs={{0,1},{1,2},{2,3},{3,0},{4,5},{5,6},{6,7},{7,4},{8,9},{9,10},{10,1... | collective-permute-start | bytes 393224 | tf_op jit(solution)/shard_map/ppermute | solution.py:76
  28.0 11.9 %collective-permute-start.2 = (bf16[128,512]{0,1:T(8,128)(2,1)S(1)}, bf16[128,512]{0,1:T(8,128)(2,1)}, u32[]{:S(2)}, u32[]{:S(2)}) collective-permute-start(bf16[128,512]{0,1:T(8,128)(2,1)S(1)} %collective-permute-done.1), channel_id=1, source_target_pairs={{0,1},{1,2},{2,3},{3,0},{4,5},{5,6},{6,7},{7,4},{8,9},{9,10},{10,1... | collective-permute-start | bytes 393224 | tf_op jit(solution)/shard_map/ppermute | solution.py:76
  31.1 5.3 %copy-start.1 = (bf16[128,4096]{1,0:T(8,128)(2,1)S(1)}, bf16[128,4096]{1,0:T(8,128)(2,1)}, u32[]{:S(2)}) copy-start(bf16[128,4096]{1,0:T(8,128)(2,1)} %param.15) | copy-start | bytes 3145732
  31.1 148.1 %all-to-all-start = ((bf16[128,64,128]{2,0,1:T(8,128)(2,1)}), bf16[128,64,128]{2,0,1:T(8,128)(2,1)S(1)}, u32[]{:S(2)}, u32[]{:S(2)}) async-start(bf16[128,64,128]{2,0,1:T(8,128)(2,1)} %select_bitcast_fusion), calls=%async_computation | async-start | bytes 4194304 | tf_op jit(solution)/shard_map/all_to_all | solution.py:89
  35.5 226.2 %all-gather.5.cloned.1.call-start = ((), (), s32[]{:S(2)}) async-start(), calls=%async_computation.2 | async-start | bytes 3604480 | tf_op jit(solution)/shard_map/all_gather | solution.py:100
  36.3 227.9 %reduce-scatter.2.cloned.1.call-start = ((), (), s32[]{:S(2)}) async-start(), calls=%async_computation.4 | async-start | bytes 4718592 | tf_op jit(solution)/shard_map/reduce_scatter | solution.py:91
  40.0 3.1 %copy-start.2 = (bf16[128,4096]{0,1:T(8,128)(2,1)S(1)}, bf16[128,4096]{0,1:T(8,128)(2,1)}, u32[]{:S(2)}) copy-start(bf16[128,4096]{0,1:T(8,128)(2,1)} %copy.74) | copy-start | bytes 3145732
  188.2 0.7 copy-start
  188.2 105.0 %all-gather.11.cloned.1.call-start = ((), (), s32[]{:S(2)}) async-start(), calls=%async_computation.6 | async-start | bytes 1310720 | tf_op jit(solution)/shard_map/all_gather | solution.py:109
Sparse Core Ops, SparseCore 0:
  10.4 111.9 all-gather.6
  123.9 76.9 all-gather.8
  202.4 59.2 all-gather.4
  266.5 26.6 all-gather.10
Sparse Core Ops, SparseCore 1:
  188.3 53.0 reduce-scatter.1
